TPU v7x, 32 devices: a whole 2x2x4 slice. The times are simulated.
32 devices in a mesh: blk: 16 (over z, x, core), head: 2 (over y).
Axes of the slice: x: 2, y: 2, z: 4, core: 2. Of those that a mesh axis runs over, the one named last changes fastest.
Arguments:
- query: bfloat16 [4096, 4096], P(('blk', 'head')), may hold values from -128 to 128
- key: bfloat16 [2048, 4096], P('blk', 'head'), may hold values from -8 to 8
- value: bfloat16 [2048, 4096], P('blk', 'head'), may hold values from -6 to 6
- d_out: bfloat16 [4096, 4096], P(('blk', 'head')), may hold values from -6 to 6
- seg_map: int32 [32], replicated, may hold values from 0 to 7, never falling along the last dimension, each value on 1 to 8 neighbouring positions
- spans: int32 [8, 8], replicated, may hold values from 0 to 15, all different within a row
Outputs:
- attn_out: bfloat16 [4096, 4096], P(('blk', 'head'))
- d_query: bfloat16 [4096, 4096], P(('blk', 'head'))
- d_key: bfloat16 [2048, 4096], P('blk', 'head')
- d_value: bfloat16 [2048, 4096], P('blk', 'head')
Inputs may be any that keep to these rules, and one draw needn't show every extreme that they name: `seg_map`: segment numbers never fall from one CAD block to the next; each segment covers 1 to 8 blocks, one exactly 8. `spans`: each row names 8 different document blocks; every document block is named by some row.
All inputs are finite; a program needn't handle non-finite values.
Results may differ from a plain program's by a relative error of at most 0.024.
Values may be sent and summed in bfloat16 or wider, within the bound.
A program may use at most 128 MiB of HBM per device.

v0:
```python
import functools
import math

import jax
import jax.numpy as jnp
from jax import lax
from jax.experimental import pallas as pl
from jax.experimental.pallas import tpu as pltpu
from jax.sharding import PartitionSpec as P

HEADS = 32
HEAD_DIM = 128
BLOCK = 128
SPANS = 8

NT = (((1,), (1,)), ((), ()))
MESH = pl.DeviceIdType.MESH


def attend_block(q, do, k_cat, v_cat, kt_cat, vt_cat, factor):
    f32 = jnp.float32
    s = lax.dot_general(k_cat, q, NT, preferred_element_type=f32)
    dp = lax.dot_general(v_cat, do, NT, preferred_element_type=f32)
    top = jnp.max(s, axis=0, keepdims=True)
    e = jnp.exp((s - top) * factor)
    inv = 1.0 / jnp.sum(e, axis=0, keepdims=True)
    p = e * inv
    delta = jnp.sum(p * dp, axis=0, keepdims=True)
    pb = p.astype(jnp.bfloat16)
    ds = (p * (dp - delta)).astype(jnp.bfloat16)
    attn_t = jnp.dot(vt_cat, pb, preferred_element_type=f32)
    dq_t = jnp.dot(kt_cat, ds, preferred_element_type=f32) * factor
    return attn_t.T.astype(jnp.bfloat16), dq_t.T.astype(jnp.bfloat16), pb, ds


def fused_kernel(
    blks, columns, parts, unroll, factor,
    seg_ref, spans_ref, q_in, do_in, k_in, v_in,
    at_out, dq_out, dk_out, dv_out,
    q_s, do_s, k_s, v_s, kn, vn, kt, vt, p_s, ds_s, at_s, dq_s, dk_s, dv_s,
    slot_ref, in_send, out_send, k_recv, v_recv, q_recv, do_recv, out_recv,
):
    count = blks * columns
    near = blks // parts
    members = near * columns
    each = HEADS // members
    docs = blks
    blk, col = lax.axis_index("blk"), lax.axis_index("head")
    part, spot = blk // near, lax.rem(blk, near)
    mine = spot * columns + col
    bf16 = jnp.bfloat16

    def cols(index):
        return pl.ds(pl.multiple_of(index * HEAD_DIM, HEAD_DIM), HEAD_DIM)

    def member(m):
        return part * near + m // columns, lax.rem(m, columns)

    def doc_head(b, h):
        return lax.rem(b, near) * each + h

    def cad_head(m, h):
        return lax.rem(m, columns) * (HEADS // columns) + m // columns * each + h

    def turn(t, size):
        half = (t + 1) // 2
        back = lax.rem(t + 1, 2)
        return lax.rem(half + back * (size - 2 * half) + size, size)

    def local(src, dst, sem):
        pltpu.make_async_copy(src, dst, sem).start()

    def remote(src, dst, send, recv, where):
        pltpu.make_async_remote_copy(
            src_ref=src, dst_ref=dst, send_sem=send, recv_sem=recv,
            device_id=where, device_id_type=MESH,
        ).start()

    barrier = pltpu.get_barrier_semaphore()

    @pl.loop(1, count)
    def _(t):
        to = lax.rem(blk * columns + col + t, count)
        where = (to // columns, lax.rem(to, columns))
        pl.semaphore_signal(barrier, inc=1, device_id=where, device_id_type=MESH)

    for h in range(each):
        doc, cad = doc_head(blk, h), cad_head(mine, h)
        local(k_in.at[:, cols(doc)], k_s.at[h * docs + blk], k_recv.at[h])
        local(v_in.at[:, cols(doc)], v_s.at[h * docs + blk], v_recv.at[h])
        at = h * members + mine
        local(q_in.at[:, cols(cad)], q_s.at[at], q_recv.at[at])
        local(do_in.at[:, cols(cad)], do_s.at[at], do_recv.at[at])
    pl.semaphore_wait(barrier, count - 1)

    @pl.loop(0, each)
    def _(h):
        @pl.loop(1, blks)
        def _(t):
            to = lax.rem(blk + turn(t, blks), blks)
            doc = cols(doc_head(to, h))
            slot = h * docs + blk
            remote(k_in.at[:, doc], k_s.at[slot], in_send.at[0], k_recv.at[h], (to, col))
            remote(v_in.at[:, doc], v_s.at[slot], in_send.at[1], v_recv.at[h], (to, col))

        @pl.loop(1, members)
        def _(t):
            m = lax.rem(mine + turn(t, members), members)
            cad = cols(cad_head(m, h))
            slot = h * members + mine
            remote(q_in.at[:, cad], q_s.at[slot], in_send.at[2], q_recv.at[slot], member(m))
            remote(do_in.at[:, cad], do_s.at[slot], in_send.at[3], do_recv.at[slot], member(m))

    @pl.loop(0, spans_ref.shape[0])
    def _(g):
        named = [spans_ref[g, j] for j in range(SPANS)]
        for d in range(docs):
            found = SPANS
            for j in range(SPANS):
                found = jnp.where(named[j] == d, j, found)
            slot_ref[g, d] = found

    @pl.loop(0, members)
    def _(m):
        p_s[m, SPANS] = jnp.zeros((BLOCK, BLOCK), bf16)
        ds_s[m, SPANS] = jnp.zeros((BLOCK, BLOCK), bf16)

    def wait_for(view, sem):
        pltpu.make_async_copy(view, view, sem).wait()

    def source(t):
        return lax.rem(mine + members - turn(t, members), members)

    pair, chunk = 2, 8

    @pl.loop(0, each)
    def _(h):
        wait_for(k_s.at[pl.ds(h * docs, docs)], k_recv.at[h])
        wait_for(v_s.at[pl.ds(h * docs, docs)], v_recv.at[h])

        @pl.loop(0, docs)
        def _(d):
            k_tile, v_tile = k_s[h * docs + d], v_s[h * docs + d]
            kn[d] = k_tile
            vn[d] = v_tile
            kt[d] = k_tile.T
            vt[d] = v_tile.T

        here = cols(cad_head(mine, h))
        there = cols(doc_head(blk, h))

        def send_rows(t):
            m = source(t)
            slot = h * members + m

            @pl.when(t == 0)
            def _():
                local(at_s.at[slot], at_out.at[:, here], out_recv.at[0])
                local(dq_s.at[slot], dq_out.at[:, here], out_recv.at[1])

            @pl.when(t > 0)
            def _():
                remote(at_s.at[slot], at_out.at[:, here], out_send.at[0], out_recv.at[0], member(m))
                remote(dq_s.at[slot], dq_out.at[:, here], out_send.at[1], out_recv.at[1], member(m))

        @pl.loop(0, members // unroll)
        def _(step):
            @pl.when(step > 0)
            def _():
                for u in range(unroll):
                    send_rows((step - 1) * unroll + u)

            for u in range(unroll):
                slot = h * members + source(step * unroll + u)
                wait_for(q_s.at[slot], q_recv.at[slot])
                wait_for(do_s.at[slot], do_recv.at[slot])
            results = []
            for u in range(unroll):
                m = source(step * unroll + u)
                slot = h * members + m
                seg = seg_ref[part * members + m]
                ids = [spans_ref[seg, j] for j in range(SPANS)]
                k_cat = jnp.concatenate([kn[i] for i in ids], axis=0)
                v_cat = jnp.concatenate([vn[i] for i in ids], axis=0)
                kt_cat = jnp.concatenate([kt[i] for i in ids], axis=1)
                vt_cat = jnp.concatenate([vt[i] for i in ids], axis=1)
                q, do = q_s[slot], do_s[slot]
                results.append((m, slot, attend_block(q, do, k_cat, v_cat, kt_cat, vt_cat, factor)))
            for m, slot, (at, dq, pb, ds) in results:
                at_s[slot] = at
                dq_s[slot] = dq
                p_s[m, 0:SPANS] = pb.reshape(SPANS, BLOCK, BLOCK)
                ds_s[m, 0:SPANS] = ds.reshape(SPANS, BLOCK, BLOCK)

        for u in range(unroll):
            send_rows(members - unroll + u)

        def send_doc(t):
            to = lax.rem(blk + turn(t, blks), blks)
            slot = h * docs + to
            dk_to, dv_to = dk_out.at[part, :, there], dv_out.at[part, :, there]

            @pl.when(t == 0)
            def _():
                local(dk_s.at[slot], dk_to, out_recv.at[2])
                local(dv_s.at[slot], dv_to, out_recv.at[3])

            @pl.when(t > 0)
            def _():
                remote(dk_s.at[slot], dk_to, out_send.at[2], out_recv.at[2], (to, col))
                remote(dv_s.at[slot], dv_to, out_send.at[3], out_recv.at[3], (to, col))

        @pl.loop(0, docs // pair)
        def _(step):
            @pl.when(step > 0)
            def _():
                for u in range(pair):
                    send_doc((step - 1) * pair + u)

            to = [lax.rem(blk + turn(step * pair + u, blks), blks) for u in range(pair)]
            for held, right, out, scale in ((ds_s, q_s, dk_s, factor), (p_s, do_s, dv_s, None)):
                total = jnp.zeros((pair * BLOCK, HEAD_DIM), jnp.float32)
                for i in range(0, members, chunk):
                    segs = [seg_ref[part * members + i + c] for c in range(chunk)]
                    left = jnp.concatenate([
                        jnp.concatenate([held[i + c, slot_ref[segs[c], d]] for c in range(chunk)], axis=1)
                        for d in to], axis=0)
                    rows = right[pl.ds(h * members + i, chunk)].reshape(chunk * BLOCK, HEAD_DIM)
                    total = total + jnp.dot(left, rows, preferred_element_type=jnp.float32)
                if scale is not None:
                    total = total * scale
                for u, d in enumerate(to):
                    out[h * docs + d] = total[u * BLOCK:(u + 1) * BLOCK].astype(bf16)

        for u in range(pair):
            send_doc(docs - pair + u)

    def drain(array, blocks, sem):
        wait_for(array.at[pl.ds(0, blocks)], sem)

    for i, array in enumerate((k_s, v_s, q_s, do_s)):
        drain(array, each * ((blks if i < 2 else members) - 1), in_send.at[i])
    for i, array in enumerate((at_s, dq_s, dk_s, dv_s)):
        drain(array, each * ((members if i < 2 else blks) - 1), out_send.at[i])
    for i, array in enumerate((at_s, dq_s, dk_s, dv_s)):
        drain(array, each * (members if i < 2 else blks), out_recv.at[i])


def finish_kernel(at_in, dq_in, dk_in, dv_in, at_ref, dq_ref, dk_ref, dv_ref):
    at_ref[...] = at_in[...]
    dq_ref[...] = dq_in[...]
    for src, dst in ((dk_in, dk_ref), (dv_in, dv_ref)):
        total = src[0].astype(jnp.float32)
        for p in range(1, src.shape[0]):
            total = total + src[p].astype(jnp.float32)
        dst[...] = total.astype(jnp.bfloat16)


def finish(at, dq, dk, dv, steps=2):
    rows, wide = at.shape
    parts, docs, narrow = dk.shape
    cad = pl.BlockSpec((rows, wide // steps), lambda i: (0, i))
    partial = pl.BlockSpec((parts, docs, narrow // steps), lambda i: (0, 0, i))
    doc = pl.BlockSpec((docs, narrow // steps), lambda i: (0, i))
    return pl.pallas_call(
        finish_kernel,
        grid=(steps,),
        out_shape=[jax.ShapeDtypeStruct(a.shape[-2:], a.dtype) for a in (at, dq, dk, dv)],
        in_specs=[cad, cad, partial, partial],
        out_specs=[cad, cad, doc, doc],
        name="finish",
    )(at, dq, dk, dv)


def body(query, key, value, d_out, seg_map, spans):
    if query.shape[0] != BLOCK or key.shape[0] != BLOCK:
        return body_shared(query, key, value, d_out, seg_map, spans)
    blks, columns = lax.axis_size("blk"), lax.axis_size("head")
    parts = 2
    docs = blks
    members = blks // parts * columns
    each = HEADS // members
    bf16 = jnp.bfloat16
    rows, tiles = (each * members, BLOCK, HEAD_DIM), (each * docs, BLOCK, HEAD_DIM)
    flipped = (docs, HEAD_DIM, BLOCK)
    held = (members, SPANS + 1, BLOCK, BLOCK)
    anywhere = pl.BlockSpec(memory_space=pl.ANY)
    scalars = pl.BlockSpec(memory_space=pltpu.SMEM)
    partial = jax.ShapeDtypeStruct((parts, *key.shape), bf16)
    cad = jax.ShapeDtypeStruct(query.shape, bf16)
    outs = pl.pallas_call(
        functools.partial(fused_kernel, blks, columns, parts, 2, 1.0 / math.sqrt(HEAD_DIM)),
        out_shape=[cad, cad, partial, partial],
        in_specs=[scalars] * 2 + [anywhere] * 4,
        out_specs=[anywhere] * 4,
        scratch_shapes=[
            pltpu.VMEM(rows, bf16), pltpu.VMEM(rows, bf16),
            pltpu.VMEM(tiles, bf16), pltpu.VMEM(tiles, bf16),
            pltpu.VMEM((docs, BLOCK, HEAD_DIM), bf16), pltpu.VMEM((docs, BLOCK, HEAD_DIM), bf16),
            pltpu.VMEM(flipped, bf16), pltpu.VMEM(flipped, bf16),
            pltpu.VMEM(held, bf16), pltpu.VMEM(held, bf16),
            pltpu.VMEM(rows, bf16), pltpu.VMEM(rows, bf16),
            pltpu.VMEM(tiles, bf16), pltpu.VMEM(tiles, bf16),
            pltpu.SMEM((spans.shape[0], docs), jnp.int32),
            pltpu.SemaphoreType.DMA((4,)), pltpu.SemaphoreType.DMA((4,)),
            pltpu.SemaphoreType.DMA((each,)), pltpu.SemaphoreType.DMA((each,)),
            pltpu.SemaphoreType.DMA((each * members,)), pltpu.SemaphoreType.DMA((each * members,)),
            pltpu.SemaphoreType.DMA((4,)),
        ],
        compiler_params=pltpu.CompilerParams(
            collective_id=0, has_side_effects=True, vmem_limit_bytes=60 << 20
        ),
        name="attend",
    )(seg_map, spans, query, d_out, key, value)
    return finish(*outs)


def fits_one_head_each(mesh):
    return mesh.shape["blk"] * mesh.shape["head"] == HEADS and mesh.shape["blk"] % 8 == 0


def head_pass(q_head, dout_head, key_head, value_head, id_groups):
    factor = 1.0 / math.sqrt(HEAD_DIM)
    group_width = q_head.shape[1]
    doc_blocks = key_head.shape[0]

    def one_group(sums, inputs):
        q_group, dout_group, group_ids = inputs
        flat_ids = group_ids.reshape(group_width * SPANS)
        key_tiles = jnp.take(key_head, flat_ids, axis=0).reshape(
            group_width, SPANS * BLOCK, HEAD_DIM
        )
        value_tiles = jnp.take(value_head, flat_ids, axis=0).reshape(
            group_width, SPANS * BLOCK, HEAD_DIM
        )
        scores = (
            jnp.einsum("cqd,ckd->cqk", q_group, key_tiles, preferred_element_type=jnp.float32)
            * factor
        )
        top_score = jnp.max(scores, axis=-1, keepdims=True)
        expo = jnp.exp(scores - top_score)
        prob = expo / jnp.sum(expo, axis=-1, keepdims=True)
        prob_b = prob.astype(jnp.bfloat16)
        attn = jnp.einsum("cqk,ckd->cqd", prob_b, value_tiles, preferred_element_type=jnp.float32)
        delta = jnp.sum(dout_group.astype(jnp.float32) * attn, axis=-1, keepdims=True)
        dprob = jnp.einsum(
            "cqd,ckd->cqk", dout_group, value_tiles, preferred_element_type=jnp.float32
        )
        dscore_b = (prob * (dprob - delta)).astype(jnp.bfloat16)
        grad_query = (
            jnp.einsum("cqk,ckd->cqd", dscore_b, key_tiles, preferred_element_type=jnp.float32)
            * factor
        ).astype(jnp.bfloat16)
        key_slots = (
            jnp.einsum("cqk,cqd->ckd", dscore_b, q_group, preferred_element_type=jnp.float32)
            * factor
        )
        value_slots = jnp.einsum(
            "cqk,cqd->ckd", prob_b, dout_group, preferred_element_type=jnp.float32
        )
        one_hot = (jnp.arange(doc_blocks, dtype=jnp.int32)[:, None] == flat_ids[None, :]).astype(
            jnp.float32
        )
        key_sums = sums[0] + jnp.dot(
            one_hot,
            key_slots.reshape(group_width * SPANS, BLOCK * HEAD_DIM),
            precision=lax.Precision.HIGHEST,
            preferred_element_type=jnp.float32,
        )
        value_sums = sums[1] + jnp.dot(
            one_hot,
            value_slots.reshape(group_width * SPANS, BLOCK * HEAD_DIM),
            precision=lax.Precision.HIGHEST,
            preferred_element_type=jnp.float32,
        )
        return ((key_sums, value_sums), (attn.astype(jnp.bfloat16), grad_query))

    zero_sums = jnp.zeros((doc_blocks, BLOCK * HEAD_DIM), jnp.float32)
    (key_sums, value_sums), (attn_head, grad_head) = lax.scan(
        one_group, (zero_sums, zero_sums), (q_head, dout_head, id_groups)
    )
    return (attn_head, grad_head, key_sums, value_sums)


def block_table(global_blocks, seg_map, spans):
    block_count = global_blocks.shape[0]
    seg_match = (
        global_blocks[:, None] == jnp.arange(seg_map.shape[0], dtype=jnp.int32)[None, :]
    ).astype(jnp.int32)
    seg_here = jnp.sum(seg_match * seg_map[None, :], axis=1)
    span_match = (seg_here[:, None] == jnp.arange(spans.shape[0], dtype=jnp.int32)[None, :]).astype(
        jnp.int32
    )
    block_ids = jnp.sum(span_match[:, :, None] * spans[None, :, :], axis=1)
    group_width = math.gcd(block_count, max(1, 512 // BLOCK))
    group_count = block_count // group_width
    return (block_ids.reshape(group_count, group_width, SPANS), group_count, group_width)


def by_heads(array, heads_count, group_count, group_width):
    block_count = group_count * group_width
    shaped = array.reshape(block_count, BLOCK, heads_count, HEAD_DIM).transpose(2, 0, 1, 3)
    return shaped.reshape(heads_count, group_count, group_width, BLOCK, HEAD_DIM)


def from_heads(array, heads_count):
    row_count = array.shape[1] * array.shape[2] * BLOCK
    shaped = array.reshape(heads_count, row_count, HEAD_DIM).transpose(1, 0, 2)
    return shaped.reshape(row_count, heads_count * HEAD_DIM)


def from_head_sums(array, heads_count):
    doc_rows = array.shape[1] // HEAD_DIM * BLOCK // BLOCK * array.shape[0] // array.shape[0]
    doc_rows = array.shape[1] * array.shape[2] // (BLOCK * HEAD_DIM) * BLOCK
    shaped = array.reshape(heads_count, doc_rows, HEAD_DIM).transpose(1, 0, 2)
    return shaped.reshape(doc_rows, heads_count * HEAD_DIM)


def body_shared(query, key, value, d_out, seg_map, spans):
    dummy_carry = jnp.zeros((), jnp.int32)
    heads_here = HEADS // lax.axis_size("blk")
    q_rows, dout_rows = (
        lax.all_to_all(query, "blk", split_axis=1, concat_axis=0, tiled=True),
        lax.all_to_all(d_out, "blk", split_axis=1, concat_axis=0, tiled=True),
    )
    per_device = query.shape[0] // BLOCK
    block_count = q_rows.shape[0] // BLOCK
    local_blocks = jnp.arange(block_count, dtype=jnp.int32)
    global_blocks = (
        local_blocks // per_device * lax.axis_size("head") + lax.axis_index("head")
    ) * per_device + local_blocks % per_device
    id_groups, group_count, group_width = block_table(global_blocks, seg_map, spans)
    q_heads = by_heads(q_rows, heads_here, group_count, group_width)
    dout_heads = by_heads(dout_rows, heads_here, group_count, group_width)
    key_wide, value_wide = (
        lax.all_gather(key, "head", axis=1, tiled=True),
        lax.all_gather(value, "head", axis=1, tiled=True),
    )
    key_cols, value_cols = (
        lax.all_to_all(key_wide, "blk", split_axis=1, concat_axis=0, tiled=True),
        lax.all_to_all(value_wide, "blk", split_axis=1, concat_axis=0, tiled=True),
    )
    doc_blocks = key_cols.shape[0] // BLOCK

    def to_blocks(array):
        return array.reshape(doc_blocks, BLOCK, heads_here, HEAD_DIM).transpose(2, 0, 1, 3)

    def scan_head(carry, inputs):
        q_head, dout_head, key_head, value_head = inputs
        return (carry, head_pass(q_head, dout_head, key_head, value_head, id_groups))

    _, (attn_heads, grad_heads, key_parts, value_parts) = lax.scan(
        scan_head, dummy_carry, (q_heads, dout_heads, to_blocks(key_cols), to_blocks(value_cols))
    )
    key_back, value_back = (
        lax.all_to_all(
            from_head_sums(key_parts, heads_here).astype(jnp.bfloat16),
            "blk",
            split_axis=0,
            concat_axis=1,
            tiled=True,
        ).astype(jnp.float32),
        lax.all_to_all(
            from_head_sums(value_parts, heads_here).astype(jnp.bfloat16),
            "blk",
            split_axis=0,
            concat_axis=1,
            tiled=True,
        ).astype(jnp.float32),
    )
    key_total, value_total = (
        lax.psum_scatter(
            key_back.astype(jnp.bfloat16), "head", scatter_dimension=1, tiled=True
        ).astype(jnp.float32),
        lax.psum_scatter(
            value_back.astype(jnp.bfloat16), "head", scatter_dimension=1, tiled=True
        ).astype(jnp.float32),
    )
    attn_out, d_query = (
        lax.all_to_all(
            from_heads(attn_heads, heads_here), "blk", split_axis=0, concat_axis=1, tiled=True
        ),
        lax.all_to_all(
            from_heads(grad_heads, heads_here), "blk", split_axis=0, concat_axis=1, tiled=True
        ),
    )
    return (attn_out, d_query, key_total.astype(jnp.bfloat16), value_total.astype(jnp.bfloat16))


def solution(mesh):
    placed = (
        P(("blk", "head"), None),
        P("blk", "head"),
        P("blk", "head"),
        P(("blk", "head"), None),
        P(),
        P(),
    )
    return jax.shard_map(
        body if fits_one_head_each(mesh) else body_shared,
        mesh=mesh,
        in_specs=placed,
        out_specs=(
            P(("blk", "head"), None),
            P(("blk", "head"), None),
            P("blk", "head"),
            P("blk", "head"),
        ),
        check_vma=False,
    )
```

profile of v0, /device:TPU:0, one launch (start us, length us, event | category | flops | bytes accessed | tf_op | source)
XLA Modules:
  0.0 127.8 jit_solution(794842173105854882)
XLA Ops:
  0.6 123.7 %attend.1 = (bf16[128,4096]{1,0:T(8,128)(2,1)}, bf16[128,4096]{1,0:T(8,128)(2,1)}, bf16[2,128,2048]{2,1,0:T(8,128)(2,1)}, bf16[2,128,2048]{2,1,0:T(8,128)(2,1)}) custom-call(s32[32]{0:T(128)} %seg_ref.1, s32[8,8]{1,0:T(8,128)} %spans_ref.1, bf16[128,4096]{1,0:T(8,128)(2,1)} %q_in.1, bf16[128,4096]{1,0:T(8,128)(2,1)} %do_in.1, bf16[128,2048]{1,0:T(8,128)(2,1)} %k_in.1, ...), custom_call_target="tpu_custom_call" | custom-call | tf_op jit(solution)/shard_map/attend/pallas_call | solution.py:291
  124.4 3.4 %finish.1 = (bf16[128,4096]{1,0:T(8,128)(2,1)}, bf16[128,4096]{1,0:T(8,128)(2,1)}, bf16[128,2048]{1,0:T(8,128)(2,1)}, bf16[128,2048]{1,0:T(8,128)(2,1)}) custom-call(bf16[128,4096]{1,0:T(8,128)(2,1)} %get-tuple-element.8.at_in, bf16[128,4096]{1,0:T(8,128)(2,1)} %get-tuple-element.9.dq_in, bf16[2,128,2048]{2,1,0:T(8,128)(2,1)} %get-tuple-element.10.dk_in, ...), custom_call_target="tpu_custom_call" | custom-call | tf_op jit(solution)/shard_map/finish/pallas_call | solution.py:265
where the time goes:
time: 128 us
  Pallas kernels  127 us (99%)
    pallas_call x1, Pallas kernels, body(): pl.pallas_call(functools.partial(fused_kernel, blks, columns, parts, 2, 1...  124 us
    pallas_call x1, Pallas kernels, finish(): pl.pallas_call(finish_kernel, grid=(steps,), out_shape=[jax.ShapeDtypeStr...  3.43 us

commit v1 on v0

v1 whole, which is shorter than its diff:
```python
import functools
import math

import jax
import jax.numpy as jnp
from jax import lax
from jax.experimental import pallas as pl
from jax.experimental.pallas import tpu as pltpu
from jax.sharding import PartitionSpec as P

HEADS = 32
HEAD_DIM = 128
BLOCK = 128
SPANS = 8
LOG2E = math.log2(math.e)

NT = (((1,), (1,)), ((), ()))
MESH = pl.DeviceIdType.MESH


def tile_sum(x, op):
    return op(x.reshape(x.shape[0] // 8, 8, x.shape[1]), axis=0)


def fused_kernel(
    blks, columns, factor,
    seg_ref, spans_ref, q_in, do_in, k_in, v_in,
    at_out, dq_out, dk_out, dv_out, dk_far, dv_far,
    q_s, do_s, k_s, v_s, kn, vn, kt, vt, p_s, ds_s, at_s, dq_s,
    xk_s, xv_s, xk_r, xv_r, dk_f, dv_f, dk_s, dv_s, s_ref, dp_ref, slot_ref,
    in_send, relay_send, x_send, out_send, far_send,
    k_recv, v_recv, kx_recv, vx_recv, q_recv, do_recv, xk_recv, xv_recv, out_recv,
):
    near = blks // 2
    lines = near // 2
    planes = blks // lines
    group = lines * columns
    members = near * columns
    share = HEADS // group
    docs = blks
    unroll, pair, chunk = 2, 2, 8
    blk, col = lax.axis_index("blk"), lax.axis_index("head")
    z, line = blk // lines, lax.rem(blk, lines)
    half = z // 2
    level = z - 2 * half
    place = line * columns + col
    mine = level * group + place
    inner = 1 - half
    is_inner = level == inner

    def inward(a_line):
        return share - 1 - lax.rem(a_line, 2)

    own = jnp.where(is_inner, inward(line), share - inward(line))

    def head_of(h):
        return line * share + jnp.where(is_inner, h, share - 1 - h)

    other = ((planes - 1 - z) * lines + line, col)
    bf16 = jnp.bfloat16

    def cols(index):
        return pl.ds(pl.multiple_of(index * HEAD_DIM, HEAD_DIM), HEAD_DIM)

    def member(m):
        return half * near + m // columns, lax.rem(m, columns)

    def turn(t, size):
        ahead = (t + 1) // 2
        back = lax.rem(t + 1, 2)
        return lax.rem(ahead + back * (size - 2 * ahead) + size, size)

    def local(src, dst, sem):
        pltpu.make_async_copy(src, dst, sem).start()

    def remote(src, dst, send, recv, where):
        pltpu.make_async_remote_copy(
            src_ref=src, dst_ref=dst, send_sem=send, recv_sem=recv,
            device_id=where, device_id_type=MESH,
        ).start()

    def wait_for(view, sem):
        pltpu.make_async_copy(view, view, sem).wait()

    barrier = pltpu.get_barrier_semaphore()

    @pl.loop(0, near)
    def _(t):
        to = ((1 - half) * near + t, col)
        pl.semaphore_signal(barrier, inc=1, device_id=to, device_id_type=MESH)

    @pl.loop(1, members)
    def _(t):
        to = member(lax.rem(mine + t, members))
        pl.semaphore_signal(barrier, inc=1, device_id=to, device_id_type=MESH)

    pl.semaphore_wait(barrier, near + members - 1)

    def place_of(j, to_line):
        inside = j < inward(to_line)
        return jnp.where(inside, inner, 1 - inner), jnp.where(inside, j, share - 1 - j)

    def send_docs(j):
        @pl.loop(0, lines)
        def _(t):
            to_line = lax.rem(line + t, lines)
            to_level, h = place_of(j, to_line)
            slot, at = h * docs + blk, h * 2 + level
            to = half * near + to_level * lines + to_line
            head = cols(to_line * share + j)

            @pl.when(to == blk)
            def _():
                local(k_in.at[:, head], k_s.at[slot], k_recv.at[at])
                local(v_in.at[:, head], v_s.at[slot], v_recv.at[at])

            @pl.when(to != blk)
            def _():
                remote(k_in.at[:, head], k_s.at[slot], in_send.at[0], k_recv.at[at], (to, col))
                remote(v_in.at[:, head], v_s.at[slot], in_send.at[1], v_recv.at[at], (to, col))

    def send_rows_in(j):
        @pl.loop(0, group)
        def _(t):
            spot = lax.rem(place + turn(t, group), group)
            to_line, to_col = spot // columns, lax.rem(spot, columns)
            to_level, h = place_of(j, to_line)
            slot = h * members + mine
            m = to_level * group + spot
            head = cols(to_col * (HEADS // columns) + to_line * share + j)

            @pl.when(m == mine)
            def _():
                local(q_in.at[:, head], q_s.at[slot], q_recv.at[slot])
                local(do_in.at[:, head], do_s.at[slot], do_recv.at[slot])

            @pl.when(m != mine)
            def _():
                remote(q_in.at[:, head], q_s.at[slot], in_send.at[2], q_recv.at[slot], member(m))
                remote(do_in.at[:, head], do_s.at[slot], in_send.at[3], do_recv.at[slot], member(m))

    def send_far(j):
        @pl.loop(0, lines)
        def _(t):
            to_line = lax.rem(line + t, lines)
            h = place_of(j, to_line)[1]
            inside = j < inward(to_line)
            to_z = jnp.where(inside, 2 - half, (planes - 1) * (1 - half))
            slot, at = h * docs + blk, h * 2 + level
            head = cols(to_line * share + j)
            to = (to_z * lines + to_line, col)

            @pl.when(jnp.logical_not(inside) | (is_inner & (j == 0)))
            def _():
                remote(k_in.at[:, head], k_s.at[slot], in_send.at[0], kx_recv.at[at], to)
                remote(v_in.at[:, head], v_s.at[slot], in_send.at[1], vx_recv.at[at], to)

    def relay(h, plane):
        at = h * 2 + plane
        rows = pl.ds(h * docs + half * near + plane * lines, lines)
        wait_for(k_s.at[rows], k_recv.at[at])
        remote(k_s.at[rows], k_s.at[rows], relay_send.at[0], kx_recv.at[at], other)
        wait_for(v_s.at[rows], v_recv.at[at])
        remote(v_s.at[rows], v_s.at[rows], relay_send.at[1], vx_recv.at[at], other)

    last = share - 1
    send_docs(0)

    @pl.when(is_inner)
    def _():
        send_far(0)

    send_docs(1)
    send_docs(last)
    send_rows_in(last)
    send_rows_in(0)

    @pl.when(is_inner)
    def _():
        relay(0, 1 - level)
        relay(1, level)
        relay(1, 1 - level)

    send_far(last)
    send_rows_in(1)
    for j in range(2, last):
        send_docs(j)
        send_far(j)
        send_rows_in(j)

    @pl.when(is_inner)
    def _():
        @pl.loop(2, own)
        def _(h):
            relay(h, level)

    @pl.loop(0, spans_ref.shape[0])
    def _(g):
        named = [spans_ref[g, j] for j in range(SPANS)]
        for d in range(docs):
            found = SPANS
            for j in range(SPANS):
                found = jnp.where(named[j] == d, j, found)
            slot_ref[g, d] = found

    @pl.loop(0, members)
    def _(m):
        p_s[m, SPANS] = jnp.zeros((BLOCK, BLOCK), bf16)
        ds_s[m, SPANS] = jnp.zeros((BLOCK, BLOCK), bf16)

    def source(t):
        far = t // group
        spot = lax.rem(place + group - turn(lax.rem(t, group), group), group)
        return lax.rem(level + far, 2) * group + spot

    def partial(h, first):
        ids = [first + u for u in range(pair)]
        outs = []
        for held, right, scale in ((ds_s, q_s, factor), (p_s, do_s, None)):
            total = jnp.zeros((pair * BLOCK, HEAD_DIM), jnp.float32)
            for i in range(0, members, chunk):
                segs = [seg_ref[half * members + i + c] for c in range(chunk)]
                left = jnp.concatenate([
                    jnp.concatenate([held[i + c, slot_ref[segs[c], d]] for c in range(chunk)], axis=1)
                    for d in ids], axis=0)
                rows = right[pl.ds(h * members + i, chunk)].reshape(chunk * BLOCK, HEAD_DIM)
                total = total + jnp.dot(left, rows, preferred_element_type=jnp.float32)
            if scale is not None:
                total = total * scale
            outs.append(total.reshape(pair, BLOCK, HEAD_DIM))
        return outs

    def send_sums(h, step, there):
        for u in range(pair):
            slot = h * near + step * pair + u
            to = half * near + step * pair + u

            @pl.when(to == blk)
            def _():
                local(dk_s.at[slot], dk_out.at[:, there], out_recv.at[2])
                local(dv_s.at[slot], dv_out.at[:, there], out_recv.at[3])

            @pl.when(to != blk)
            def _():
                remote(dk_s.at[slot], dk_out.at[:, there], out_send.at[2], out_recv.at[2], (to, col))
                remote(dv_s.at[slot], dv_out.at[:, there], out_send.at[3], out_recv.at[3], (to, col))

    def finalize(h):
        there = cols(head_of(h))

        @pl.loop(0, near // pair)
        def _(step):
            at = h * (near // pair) + step
            rows = pl.ds(h * near + step * pair, pair)
            part = pl.ds(step * pair, pair)
            wait_for(xk_r.at[rows], xk_recv.at[at])
            wait_for(xv_r.at[rows], xv_recv.at[at])
            dk_s[rows] = (dk_f[part] + xk_r[rows].astype(jnp.float32)).astype(bf16)
            dv_s[rows] = (dv_f[part] + xv_r[rows].astype(jnp.float32)).astype(bf16)
            send_sums(h, step, there)

    steps = members // unroll

    @pl.loop(0, own)
    def _(h):
        for plane in range(2):
            rows = pl.ds(h * docs + half * near + plane * lines, lines)

            @pl.when(jnp.logical_not(is_inner) | ((plane == level) & (h == 0)))
            def _():
                wait_for(k_s.at[rows], k_recv.at[h * 2 + plane])
                wait_for(v_s.at[rows], v_recv.at[h * 2 + plane])

        for plane in range(2):
            rows = pl.ds(h * docs + (1 - half) * near + plane * lines, lines)
            wait_for(k_s.at[rows], kx_recv.at[h * 2 + plane])
            wait_for(v_s.at[rows], vx_recv.at[h * 2 + plane])

        @pl.loop(0, docs)
        def _(d):
            k_tile, v_tile = k_s[h * docs + d], v_s[h * docs + d]
            kn[d] = k_tile
            vn[d] = v_tile
            kt[d] = k_tile.T
            vt[d] = v_tile.T

        here = cols(col * (HEADS // columns) + head_of(h))

        def send_rows(t):
            m = source(t)
            slot = h * members + m

            @pl.when(m == mine)
            def _():
                local(at_s.at[slot], at_out.at[:, here], out_recv.at[0])
                local(dq_s.at[slot], dq_out.at[:, here], out_recv.at[1])

            @pl.when(m != mine)
            def _():
                remote(at_s.at[slot], at_out.at[:, here], out_send.at[0], out_recv.at[0], member(m))
                remote(dq_s.at[slot], dq_out.at[:, here], out_send.at[1], out_recv.at[1], member(m))

        @pl.loop(0, steps)
        def _(step):
            @pl.when(step > 0)
            def _():
                for u in range(unroll):
                    send_rows((step - 1) * unroll + u)

            @pl.when((step == 5) & (h > 0) & (h + 1 < own) & is_inner)
            def _():
                relay(h + 1, 1 - level)

            @pl.when((step == steps - 2) & (h > 0))
            def _():
                finalize(h - 1)

            for u in range(unroll):
                slot = h * members + source(step * unroll + u)
                wait_for(q_s.at[slot], q_recv.at[slot])
                wait_for(do_s.at[slot], do_recv.at[slot])
            f32 = jnp.float32
            which = [source(step * unroll + u) for u in range(unroll)]
            slots = [h * members + m for m in which]
            named = [[spans_ref[seg_ref[half * members + m], j] for j in range(SPANS)] for m in which]
            tops, invs, deltas = [], [], []
            for u in range(unroll):
                k_cat = jnp.concatenate([kn[i] for i in named[u]], axis=0)
                s = lax.dot_general(k_cat, q_s[slots[u]], NT, preferred_element_type=f32)
                s_ref[u] = s
                tops.append(jnp.max(tile_sum(s, jnp.max), axis=0, keepdims=True))
            for u in range(unroll):
                v_cat = jnp.concatenate([vn[i] for i in named[u]], axis=0)
                dp_ref[u] = lax.dot_general(v_cat, do_s[slots[u]], NT, preferred_element_type=f32)
            for u in range(unroll):
                total = jnp.zeros((8, BLOCK), f32)
                mixed = jnp.zeros((8, BLOCK), f32)
                for j in range(SPANS):
                    part = pl.ds(j * BLOCK, BLOCK)
                    e = jnp.exp2((s_ref[u, part] - tops[u]) * (factor * LOG2E))
                    s_ref[u, part] = e
                    total = total + tile_sum(e, jnp.sum)
                    mixed = mixed + tile_sum(e * dp_ref[u, part], jnp.sum)
                inv = 1.0 / jnp.sum(total, axis=0, keepdims=True)
                invs.append(inv)
                deltas.append(jnp.sum(mixed, axis=0, keepdims=True) * inv)
            for u in range(unroll):
                for j in range(SPANS):
                    part = pl.ds(j * BLOCK, BLOCK)
                    p = s_ref[u, part] * invs[u]
                    p_s[which[u], j] = p.astype(bf16)
                    ds_s[which[u], j] = (p * (dp_ref[u, part] - deltas[u])).astype(bf16)
            for u in range(unroll):
                vt_cat = jnp.concatenate([vt[i] for i in named[u]], axis=1)
                kt_cat = jnp.concatenate([kt[i] for i in named[u]], axis=1)
                pb = p_s[which[u], 0:SPANS].reshape(SPANS * BLOCK, BLOCK)
                ds = ds_s[which[u], 0:SPANS].reshape(SPANS * BLOCK, BLOCK)
                attn_t = jnp.dot(vt_cat, pb, preferred_element_type=f32)
                dq_t = jnp.dot(kt_cat, ds, preferred_element_type=f32) * factor
                at_s[slots[u]] = attn_t.T.astype(bf16)
                dq_s[slots[u]] = dq_t.T.astype(bf16)

        for u in range(unroll):
            send_rows(members - unroll + u)

        is_last = h == own - 1
        there = cols(head_of(h))
        beside = cols(line * 2 + jnp.where(is_inner, 0, 1))

        def send_partial(step):
            rows = pl.ds(h * near + step * pair, pair)
            at = h * (near // pair) + step

            @pl.when(jnp.logical_not(is_last))
            def _():
                remote(xk_s.at[rows], xk_r.at[rows], x_send.at[0], xk_recv.at[at], other)
                remote(xv_s.at[rows], xv_r.at[rows], x_send.at[1], xv_recv.at[at], other)

            @pl.when(is_last)
            def _():
                for u in range(pair):
                    slot = h * near + step * pair + u
                    to = ((1 - half) * near + step * pair + u, col)
                    remote(xk_s.at[slot], dk_far.at[:, beside], far_send.at[0], out_recv.at[4], to)
                    remote(xv_s.at[slot], dv_far.at[:, beside], far_send.at[1], out_recv.at[5], to)

        @pl.loop(0, near // pair)
        def _(step):
            @pl.when(step > 0)
            def _():
                send_partial(step - 1)

            rows = pl.ds(h * near + step * pair, pair)
            dk, dv = partial(h, (1 - half) * near + step * pair)
            xk_s[rows] = dk.astype(bf16)
            xv_s[rows] = dv.astype(bf16)

        send_partial(near // pair - 1)

        @pl.loop(0, near // pair)
        def _(step):
            part = pl.ds(step * pair, pair)
            dk, dv = partial(h, half * near + step * pair)

            @pl.when(jnp.logical_not(is_last))
            def _():
                dk_f[part] = dk
                dv_f[part] = dv

            @pl.when(is_last)
            def _():
                rows = pl.ds(h * near + step * pair, pair)
                dk_s[rows] = dk.astype(bf16)
                dv_s[rows] = dv.astype(bf16)
                send_sums(h, step, there)

    outward = sum(1 + a_line % 2 for a_line in range(lines))

    def drain(array, blocks, sem):
        if blocks:
            wait_for(array.at[pl.ds(0, blocks)], sem)

    def drain_sends(count, inside):
        far = outward + (lines if inside else 0)
        for i, array in enumerate((k_s, v_s)):
            drain(array, HEADS // columns - count + far, in_send.at[i])
            drain(array, (2 * count - 1) * lines if inside else 0, relay_send.at[i])
        for i, array in enumerate((q_s, do_s)):
            drain(array, HEADS - count, in_send.at[2 + i])
        for i, array in enumerate((xk_s, xv_s)):
            drain(array, (count - 1) * near, x_send.at[i])
            drain(array, near, far_send.at[i])
        for i, array in enumerate((at_s, dq_s, dk_s, dv_s)):
            drain(array, count * ((members if i < 2 else near) - 1), out_send.at[i])

    for count in range(1, share):
        @pl.when((own == count) & is_inner)
        def _():
            drain_sends(count, True)

        @pl.when((own == count) & jnp.logical_not(is_inner))
        def _():
            drain_sends(count, False)

    for i, array in enumerate((at_s, dq_s, dk_s, dv_s, xk_s, xv_s)):
        drain(array, (HEADS, HEADS // columns, 2 * lines)[i // 2], out_recv.at[i])


def finish_kernel(at_in, dq_in, dk_in, dv_in, dk_far, dv_far, at_ref, dq_ref, dk_ref, dv_ref):
    at_ref[...] = at_in[...]
    dq_ref[...] = dq_in[...]
    pairs = dk_far.shape[1] // (2 * HEAD_DIM)
    share = dk_in.shape[1] // (pairs * HEAD_DIM)
    for src, far, dst in ((dk_in, dk_far, dk_ref), (dv_in, dv_far, dv_ref)):
        for p in range(pairs):
            for j in range(share):
                here = pl.ds((p * share + j) * HEAD_DIM, HEAD_DIM)
                tile = src[:, here]
                inward = share - 1 - p % 2
                if j in (inward - 1, inward):
                    there = pl.ds((p * 2 + j - inward + 1) * HEAD_DIM, HEAD_DIM)
                    total = tile.astype(jnp.float32) + far[:, there].astype(jnp.float32)
                    tile = total.astype(jnp.bfloat16)
                dst[:, here] = tile


def finish(*arrays, steps=2):
    specs = [pl.BlockSpec((a.shape[0], a.shape[1] // steps), lambda i: (0, i)) for a in arrays]
    return pl.pallas_call(
        finish_kernel,
        grid=(steps,),
        out_shape=[jax.ShapeDtypeStruct(a.shape, a.dtype) for a in arrays[:4]],
        in_specs=specs,
        out_specs=specs[:4],
        name="finish",
    )(*arrays)


def body(query, key, value, d_out, seg_map, spans):
    if query.shape[0] != BLOCK or key.shape[0] != BLOCK:
        return body_shared(query, key, value, d_out, seg_map, spans)
    blks, columns = lax.axis_size("blk"), lax.axis_size("head")
    near = blks // 2
    docs, members = blks, near * columns
    most = HEADS // (near // 2 * columns) - 1
    bf16, f32 = jnp.bfloat16, jnp.float32
    dma = pltpu.SemaphoreType.DMA

    def tiles(count, kind=bf16):
        return pltpu.VMEM((count, BLOCK, HEAD_DIM), kind)

    held = pltpu.VMEM((members, SPANS + 1, BLOCK, BLOCK), bf16)
    beside = jax.ShapeDtypeStruct((key.shape[0], near * HEAD_DIM), bf16)
    anywhere = pl.BlockSpec(memory_space=pl.ANY)
    scalars = pl.BlockSpec(memory_space=pltpu.SMEM)
    outs = pl.pallas_call(
        functools.partial(fused_kernel, blks, columns, 1.0 / math.sqrt(HEAD_DIM)),
        out_shape=[jax.ShapeDtypeStruct(a.shape, bf16) for a in (query, query, key, value)] + [beside] * 2,
        in_specs=[scalars] * 2 + [anywhere] * 4,
        out_specs=[anywhere] * 6,
        scratch_shapes=[
            tiles(most * members), tiles(most * members),
            tiles(most * docs), tiles(most * docs),
            tiles(docs), tiles(docs), tiles(docs), tiles(docs),
            held, held,
            tiles(most * members), tiles(most * members),
            tiles(most * near), tiles(most * near),
            tiles(most * near), tiles(most * near),
            tiles(near, f32), tiles(near, f32),
            tiles(most * near), tiles(most * near),
            pltpu.VMEM((2, SPANS * BLOCK, BLOCK), f32), pltpu.VMEM((2, SPANS * BLOCK, BLOCK), f32),
            pltpu.SMEM((spans.shape[0], docs), jnp.int32),
            dma((4,)), dma((2,)), dma((2,)), dma((4,)), dma((2,)),
            dma((most * 2,)), dma((most * 2,)), dma((most * 2,)), dma((most * 2,)),
            dma((most * members,)), dma((most * members,)),
            dma((most * near // 2,)), dma((most * near // 2,)),
            dma((6,)),
        ],
        compiler_params=pltpu.CompilerParams(
            collective_id=0, has_side_effects=True, vmem_limit_bytes=60 << 20
        ),
        name="attend",
    )(seg_map, spans, query, d_out, key, value)
    return finish(*outs)


def fits_one_head_each(mesh):
    return mesh.shape["blk"] * mesh.shape["head"] == HEADS and mesh.shape["blk"] % 8 == 0


def head_pass(q_head, dout_head, key_head, value_head, id_groups):
    factor = 1.0 / math.sqrt(HEAD_DIM)
    group_width = q_head.shape[1]
    doc_blocks = key_head.shape[0]

    def one_group(sums, inputs):
        q_group, dout_group, group_ids = inputs
        flat_ids = group_ids.reshape(group_width * SPANS)
        key_tiles = jnp.take(key_head, flat_ids, axis=0).reshape(
            group_width, SPANS * BLOCK, HEAD_DIM
        )
        value_tiles = jnp.take(value_head, flat_ids, axis=0).reshape(
            group_width, SPANS * BLOCK, HEAD_DIM
        )
        scores = (
            jnp.einsum("cqd,ckd->cqk", q_group, key_tiles, preferred_element_type=jnp.float32)
            * factor
        )
        top_score = jnp.max(scores, axis=-1, keepdims=True)
        expo = jnp.exp(scores - top_score)
        prob = expo / jnp.sum(expo, axis=-1, keepdims=True)
        prob_b = prob.astype(jnp.bfloat16)
        attn = jnp.einsum("cqk,ckd->cqd", prob_b, value_tiles, preferred_element_type=jnp.float32)
        delta = jnp.sum(dout_group.astype(jnp.float32) * attn, axis=-1, keepdims=True)
        dprob = jnp.einsum(
            "cqd,ckd->cqk", dout_group, value_tiles, preferred_element_type=jnp.float32
        )
        dscore_b = (prob * (dprob - delta)).astype(jnp.bfloat16)
        grad_query = (
            jnp.einsum("cqk,ckd->cqd", dscore_b, key_tiles, preferred_element_type=jnp.float32)
            * factor
        ).astype(jnp.bfloat16)
        key_slots = (
            jnp.einsum("cqk,cqd->ckd", dscore_b, q_group, preferred_element_type=jnp.float32)
            * factor
        )
        value_slots = jnp.einsum(
            "cqk,cqd->ckd", prob_b, dout_group, preferred_element_type=jnp.float32
        )
        one_hot = (jnp.arange(doc_blocks, dtype=jnp.int32)[:, None] == flat_ids[None, :]).astype(
            jnp.float32
        )
        key_sums = sums[0] + jnp.dot(
            one_hot,
            key_slots.reshape(group_width * SPANS, BLOCK * HEAD_DIM),
            precision=lax.Precision.HIGHEST,
            preferred_element_type=jnp.float32,
        )
        value_sums = sums[1] + jnp.dot(
            one_hot,
            value_slots.reshape(group_width * SPANS, BLOCK * HEAD_DIM),
            precision=lax.Precision.HIGHEST,
            preferred_element_type=jnp.float32,
        )
        return ((key_sums, value_sums), (attn.astype(jnp.bfloat16), grad_query))

    zero_sums = jnp.zeros((doc_blocks, BLOCK * HEAD_DIM), jnp.float32)
    (key_sums, value_sums), (attn_head, grad_head) = lax.scan(
        one_group, (zero_sums, zero_sums), (q_head, dout_head, id_groups)
    )
    return (attn_head, grad_head, key_sums, value_sums)


def block_table(global_blocks, seg_map, spans):
    block_count = global_blocks.shape[0]
    seg_match = (
        global_blocks[:, None] == jnp.arange(seg_map.shape[0], dtype=jnp.int32)[None, :]
    ).astype(jnp.int32)
    seg_here = jnp.sum(seg_match * seg_map[None, :], axis=1)
    span_match = (seg_here[:, None] == jnp.arange(spans.shape[0], dtype=jnp.int32)[None, :]).astype(
        jnp.int32
    )
    block_ids = jnp.sum(span_match[:, :, None] * spans[None, :, :], axis=1)
    group_width = math.gcd(block_count, max(1, 512 // BLOCK))
    group_count = block_count // group_width
    return (block_ids.reshape(group_count, group_width, SPANS), group_count, group_width)


def by_heads(array, heads_count, group_count, group_width):
    block_count = group_count * group_width
    shaped = array.reshape(block_count, BLOCK, heads_count, HEAD_DIM).transpose(2, 0, 1, 3)
    return shaped.reshape(heads_count, group_count, group_width, BLOCK, HEAD_DIM)


def from_heads(array, heads_count):
    row_count = array.shape[1] * array.shape[2] * BLOCK
    shaped = array.reshape(heads_count, row_count, HEAD_DIM).transpose(1, 0, 2)
    return shaped.reshape(row_count, heads_count * HEAD_DIM)


def from_head_sums(array, heads_count):
    doc_rows = array.shape[1] // HEAD_DIM * BLOCK // BLOCK * array.shape[0] // array.shape[0]
    doc_rows = array.shape[1] * array.shape[2] // (BLOCK * HEAD_DIM) * BLOCK
    shaped = array.reshape(heads_count, doc_rows, HEAD_DIM).transpose(1, 0, 2)
    return shaped.reshape(doc_rows, heads_count * HEAD_DIM)


def body_shared(query, key, value, d_out, seg_map, spans):
    dummy_carry = jnp.zeros((), jnp.int32)
    heads_here = HEADS // lax.axis_size("blk")
    q_rows, dout_rows = (
        lax.all_to_all(query, "blk", split_axis=1, concat_axis=0, tiled=True),
        lax.all_to_all(d_out, "blk", split_axis=1, concat_axis=0, tiled=True),
    )
    per_device = query.shape[0] // BLOCK
    block_count = q_rows.shape[0] // BLOCK
    local_blocks = jnp.arange(block_count, dtype=jnp.int32)
    global_blocks = (
        local_blocks // per_device * lax.axis_size("head") + lax.axis_index("head")
    ) * per_device + local_blocks % per_device
    id_groups, group_count, group_width = block_table(global_blocks, seg_map, spans)
    q_heads = by_heads(q_rows, heads_here, group_count, group_width)
    dout_heads = by_heads(dout_rows, heads_here, group_count, group_width)
    key_wide, value_wide = (
        lax.all_gather(key, "head", axis=1, tiled=True),
        lax.all_gather(value, "head", axis=1, tiled=True),
    )
    key_cols, value_cols = (
        lax.all_to_all(key_wide, "blk", split_axis=1, concat_axis=0, tiled=True),
        lax.all_to_all(value_wide, "blk", split_axis=1, concat_axis=0, tiled=True),
    )
    doc_blocks = key_cols.shape[0] // BLOCK

    def to_blocks(array):
        return array.reshape(doc_blocks, BLOCK, heads_here, HEAD_DIM).transpose(2, 0, 1, 3)

    def scan_head(carry, inputs):
        q_head, dout_head, key_head, value_head = inputs
        return (carry, head_pass(q_head, dout_head, key_head, value_head, id_groups))

    _, (attn_heads, grad_heads, key_parts, value_parts) = lax.scan(
        scan_head, dummy_carry, (q_heads, dout_heads, to_blocks(key_cols), to_blocks(value_cols))
    )
    key_back, value_back = (
        lax.all_to_all(
            from_head_sums(key_parts, heads_here).astype(jnp.bfloat16),
            "blk",
            split_axis=0,
            concat_axis=1,
            tiled=True,
        ).astype(jnp.float32),
        lax.all_to_all(
            from_head_sums(value_parts, heads_here).astype(jnp.bfloat16),
            "blk",
            split_axis=0,
            concat_axis=1,
            tiled=True,
        ).astype(jnp.float32),
    )
    key_total, value_total = (
        lax.psum_scatter(
            key_back.astype(jnp.bfloat16), "head", scatter_dimension=1, tiled=True
        ).astype(jnp.float32),
        lax.psum_scatter(
            value_back.astype(jnp.bfloat16), "head", scatter_dimension=1, tiled=True
        ).astype(jnp.float32),
    )
    attn_out, d_query = (
        lax.all_to_all(
            from_heads(attn_heads, heads_here), "blk", split_axis=0, concat_axis=1, tiled=True
        ),
        lax.all_to_all(
            from_heads(grad_heads, heads_here), "blk", split_axis=0, concat_axis=1, tiled=True
        ),
    )
    return (attn_out, d_query, key_total.astype(jnp.bfloat16), value_total.astype(jnp.bfloat16))


def solution(mesh):
    placed = (
        P(("blk", "head"), None),
        P("blk", "head"),
        P("blk", "head"),
        P(("blk", "head"), None),
        P(),
        P(),
    )
    return jax.shard_map(
        body if fits_one_head_each(mesh) else body_shared,
        mesh=mesh,
        in_specs=placed,
        out_specs=(
            P(("blk", "head"), None),
            P(("blk", "head"), None),
            P("blk", "head"),
            P("blk", "head"),
        ),
        check_vma=False,
    )
```

time: 128 us -> 117 us (0.914); the launches traced: 128 us -> 115 us
  Pallas kernels: 127 us -> 115 us
    pallas_call x1, Pallas kernels: 124 us -> 112 us  [body(): pl.pallas_call(functools.partial(fused_kernel, blks, columns, 1.0 / math....]
where the time goes in v1:
time: 117 us; the launch traced here: 115 us
  Pallas kernels  115 us (98%)
    pallas_call x1, Pallas kernels, body(): pl.pallas_call(functools.partial(fused_kernel, blks, columns, 1.0 / math....  112 us
    pallas_call x1, Pallas kernels, finish(): pl.pallas_call(finish_kernel, grid=(steps,), out_shape=[jax.ShapeDtypeStr...  3.26 us

profile of v1, /device:TPU:0, one launch (start us, length us, event | category | flops | bytes accessed | tf_op | source)
XLA Modules:
  0.0 115.4 jit_solution(3315053717012715518)
XLA Ops:
  0.6 111.5 %attend.1 = (bf16[128,4096]{1,0:T(8,128)(2,1)}, bf16[128,4096]{1,0:T(8,128)(2,1)}, bf16[128,2048]{1,0:T(8,128)(2,1)}, bf16[128,2048]{1,0:T(8,128)(2,1)}, bf16[12...) custom-call(s32[32]{0:T(128)} %seg_ref.1, s32[8,8]{1,0:T(8,128)} %spans_ref.1, bf16[128,4096]{1,0:T(8,128)(2,1)} %q_in.1, ...), custom_call_target="tpu_custom_call" | custom-call | tf_op jit(solution)/shard_map/attend/pallas_call | solution.py:496
  112.2 3.3 %finish.1 = (bf16[128,4096]{1,0:T(8,128)(2,1)}, bf16[128,4096]{1,0:T(8,128)(2,1)}, bf16[128,2048]{1,0:T(8,128)(2,1)}, bf16[128,2048]{1,0:T(8,128)(2,1)}) custom-call(bf16[128,4096]{1,0:T(8,128)(2,1)} %get-tuple-element.10.at_in, bf16[128,4096]{1,0:T(8,128)(2,1)} %get-tuple-element.11.dq_in, bf16[128,2048]{1,0:T(8,128)(2,1)} %get-tuple-element.12.dk_in, ...), custom_call_target="tpu_custom_call" | custom-call | tf_op jit(solution)/shard_map/finish/pallas_call | solution.py:469

commit v2 on v1

--- a/solution.py
+++ b/solution.py
@@ -38,7 +38,7 @@
     members = near * columns
     share = HEADS // group
     docs = blks
-    unroll, pair, chunk = 2, 2, 8
+    unroll, pair, chunk = 2, 4, 8
     blk, col = lax.axis_index("blk"), lax.axis_index("head")
     z, line = blk // lines, lax.rem(blk, lines)
     half = z // 2
@@ -172,8 +172,11 @@
 
     send_docs(1)
     send_docs(last)
+    for j in range(2, last):
+        send_docs(j)
+        send_far(j)
+    send_rows_in(0)
     send_rows_in(last)
-    send_rows_in(0)
 
     @pl.when(is_inner)
     def _():
@@ -184,8 +187,6 @@
     send_far(last)
     send_rows_in(1)
     for j in range(2, last):
-        send_docs(j)
-        send_far(j)
         send_rows_in(j)
 
     @pl.when(is_inner)
@@ -307,13 +308,9 @@
                 for u in range(unroll):
                     send_rows((step - 1) * unroll + u)
 
-            @pl.when((step == 5) & (h > 0) & (h + 1 < own) & is_inner)
+            @pl.when((step == 7) & (h > 0) & (h + 1 < own) & is_inner)
             def _():
                 relay(h + 1, 1 - level)
-
-            @pl.when((step == steps - 2) & (h > 0))
-            def _():
-                finalize(h - 1)
 
             for u in range(unroll):
                 slot = h * members + source(step * unroll + u)
@@ -397,6 +394,10 @@
 
         send_partial(near // pair - 1)
 
+        @pl.when(h > 0)
+        def _():
+            finalize(h - 1)
+
         @pl.loop(0, near // pair)
         def _(step):
             part = pl.ds(step * pair, pair)
@@ -513,7 +514,7 @@
             dma((4,)), dma((2,)), dma((2,)), dma((4,)), dma((2,)),
             dma((most * 2,)), dma((most * 2,)), dma((most * 2,)), dma((most * 2,)),
             dma((most * members,)), dma((most * members,)),
-            dma((most * near // 2,)), dma((most * near // 2,)),
+            dma((most * near // 4,)), dma((most * near // 4,)),
             dma((6,)),
         ],
         compiler_params=pltpu.CompilerParams(

time: 117 us -> 114 us (0.974)
  Pallas kernels: 115 us -> 113 us
    pallas_call x1, Pallas kernels: 112 us -> 109 us  [body(): pl.pallas_call(functools.partial(fused_kernel, blks, columns, 1.0 / math....]
where the time goes in v2:
time: 114 us; the launch traced here: 113 us
  Pallas kernels  113 us (99%)
    pallas_call x1, Pallas kernels, body(): pl.pallas_call(functools.partial(fused_kernel, blks, columns, 1.0 / math....  109 us
    pallas_call x1, Pallas kernels, finish(): pl.pallas_call(finish_kernel, grid=(steps,), out_shape=[jax.ShapeDtypeStr...  3.26 us

profile of v2, /device:TPU:0, one launch (start us, length us, event | category | flops | bytes accessed | tf_op | source)
XLA Modules:
  0.0 113.4 jit_solution(4252641915657717752)
XLA Ops:
  0.6 109.5 %attend.1 = (bf16[128,4096]{1,0:T(8,128)(2,1)}, bf16[128,4096]{1,0:T(8,128)(2,1)}, bf16[128,2048]{1,0:T(8,128)(2,1)}, bf16[128,2048]{1,0:T(8,128)(2,1)}, bf16[12...) custom-call(s32[32]{0:T(128)} %seg_ref.1, s32[8,8]{1,0:T(8,128)} %spans_ref.1, bf16[128,4096]{1,0:T(8,128)(2,1)} %q_in.1, ...), custom_call_target="tpu_custom_call" | custom-call | tf_op jit(solution)/shard_map/attend/pallas_call | solution.py:497
  110.1 3.3 %finish.1 = (bf16[128,4096]{1,0:T(8,128)(2,1)}, bf16[128,4096]{1,0:T(8,128)(2,1)}, bf16[128,2048]{1,0:T(8,128)(2,1)}, bf16[128,2048]{1,0:T(8,128)(2,1)}) custom-call(bf16[128,4096]{1,0:T(8,128)(2,1)} %get-tuple-element.10.at_in, bf16[128,4096]{1,0:T(8,128)(2,1)} %get-tuple-element.11.dq_in, bf16[128,2048]{1,0:T(8,128)(2,1)} %get-tuple-element.12.dk_in, ...), custom_call_target="tpu_custom_call" | custom-call | tf_op jit(solution)/shard_map/finish/pallas_call | solution.py:470

commit v3 on v2

--- a/solution.py
+++ b/solution.py
@@ -308,9 +308,11 @@
                 for u in range(unroll):
                     send_rows((step - 1) * unroll + u)
 
-            @pl.when((step == 7) & (h > 0) & (h + 1 < own) & is_inner)
-            def _():
-                relay(h + 1, 1 - level)
+            @pl.when((step == 2) & (h == 0) & is_inner)
+            def _():
+                @pl.loop(2, own)
+                def _(later):
+                    relay(later, 1 - level)
 
             for u in range(unroll):
                 slot = h * members + source(step * unroll + u)

time: 114 us -> 114 us (level)
  no operation moved by 1% of the time
where the time goes in v3:
time: 114 us; the launch traced here: 113 us
  Pallas kernels  113 us (99%)
    pallas_call x1, Pallas kernels, body(): pl.pallas_call(functools.partial(fused_kernel, blks, columns, 1.0 / math....  110 us
    pallas_call x1, Pallas kernels, finish(): pl.pallas_call(finish_kernel, grid=(steps,), out_shape=[jax.ShapeDtypeStr...  3.26 us

profile of v3, /device:TPU:0, one launch (start us, length us, event | category | flops | bytes accessed | tf_op | source)
XLA Modules:
  0.0 113.4 jit_solution(13772151578100412033)
XLA Ops:
  0.6 109.5 %attend.1 = (bf16[128,4096]{1,0:T(8,128)(2,1)}, bf16[128,4096]{1,0:T(8,128)(2,1)}, bf16[128,2048]{1,0:T(8,128)(2,1)}, bf16[128,2048]{1,0:T(8,128)(2,1)}, bf16[12...) custom-call(s32[32]{0:T(128)} %seg_ref.1, s32[8,8]{1,0:T(8,128)} %spans_ref.1, bf16[128,4096]{1,0:T(8,128)(2,1)} %q_in.1, ...), custom_call_target="tpu_custom_call" | custom-call | tf_op jit(solution)/shard_map/attend/pallas_call | solution.py:499
  110.2 3.3 %finish.1 = (bf16[128,4096]{1,0:T(8,128)(2,1)}, bf16[128,4096]{1,0:T(8,128)(2,1)}, bf16[128,2048]{1,0:T(8,128)(2,1)}, bf16[128,2048]{1,0:T(8,128)(2,1)}) custom-call(bf16[128,4096]{1,0:T(8,128)(2,1)} %get-tuple-element.10.at_in, bf16[128,4096]{1,0:T(8,128)(2,1)} %get-tuple-element.11.dq_in, bf16[128,2048]{1,0:T(8,128)(2,1)} %get-tuple-element.12.dk_in, ...), custom_call_target="tpu_custom_call" | custom-call | tf_op jit(solution)/shard_map/finish/pallas_call | solution.py:472
